TPU v7x, 32 devices: a whole 2x2x4 slice. The times are simulated.
32 devices in a mesh: shard: 16 (over z, x, core), replica: 2 (over y).
Axes of the slice: x: 2, y: 2, z: 4, core: 2. Of those that a mesh axis runs over, the one named last changes fastest.
Arguments:
- x_in: bfloat16 [2, 8192, 768], P('replica', 'shard'), may hold values from -6 to 6
- seq_units: int32 [2, 16], P('replica'), may hold values from 1 to 64, 512 in all within a row
- deal: int32 [2, 16], P('replica'), may hold values from 0 to 15, each once within a row
- gain_attn: float32 [768], replicated, may hold values from 0.1 to 1.9
- w_query: bfloat16 [768, 768], P('shard'), may hold values from -0.4375 to 0.4375
- w_key: bfloat16 [768, 768], P('shard'), may hold values from -0.21875 to 0.21875
- w_value: bfloat16 [768, 768], P('shard'), may hold values from -0.21875 to 0.21875
- w_out: bfloat16 [768, 768], P('shard'), may hold values from -0.875 to 0.875
- gain_ffn: float32 [768], replicated, may hold values from 0.1 to 1.9
- w_gate: bfloat16 [768, 2048], P('shard'), may hold values from -0.21875 to 0.21875
- w_up: bfloat16 [768, 2048], P('shard'), may hold values from -0.21875 to 0.21875
- w_down: bfloat16 [2048, 768], P('shard'), may hold values from -0.125 to 0.125
- d_out: bfloat16 [2, 16, 1024, 768], P('replica', 'shard'), may hold values from -6 to 6
Outputs:
- layer_out: bfloat16 [2, 16, 1024, 768], P('replica', 'shard')
- grad_x: bfloat16 [2, 8192, 768], P('replica', 'shard')
- grad_gain_attn: float32 [768], P('shard')
- grad_gain_ffn: float32 [768], P('shard')
- grad_w_query: float32 [768, 768], P('shard')
- grad_w_key: float32 [768, 768], P('shard')
- grad_w_value: float32 [768, 768], P('shard')
- grad_w_out: float32 [768, 768], P('shard')
- grad_w_gate: float32 [768, 2048], P('shard')
- grad_w_up: float32 [768, 2048], P('shard')
- grad_w_down: float32 [2048, 768], P('shard')
Inputs may be any that keep to these rules, and one draw needn't show every extreme that they name: `seq_units`: each group's 16 entries sum to 512. `deal`: each group's row names every sequence 0 to 15 once.
All inputs are finite; a program needn't handle non-finite values.
Results may differ from a plain program's by a relative error of at most 0.023.
Values may be sent and summed in bfloat16 or wider, within the bound.
No kernel may reach another device: no remote copies, remote signals or barrier semaphores. Data moves between devices by JAX's collectives and lax.ppermute only.
A program may use at most 320 MiB of HBM per device.

v0:
```python
import jax
import jax.numpy as jnp
from jax import lax
from jax.sharding import PartitionSpec as P

H = 12
HD = 64
norm_eps = 1e-06
neg_big = -1e30


def rms_scale(tok_rows, gain_vec):
    inverse = lax.rsqrt(jnp.mean(tok_rows * tok_rows, axis=-1, keepdims=True) + norm_eps)
    return tok_rows * inverse * gain_vec


def gelu_mix(gate_vals, up_vals):
    return jax.nn.gelu(gate_vals, approximate=True) * up_vals


def lookup(table, wanted):
    table_slots = jnp.arange(table.shape[0], dtype=jnp.int32)
    return jnp.sum(jnp.where(wanted[:, None] == table_slots[None, :], table[None, :], 0), axis=1)


def left_dot(lhs_mat, rhs_mat):
    return lax.dot_general(
        lhs_mat, rhs_mat, (((0,), (0,)), ((), ())), preferred_element_type=jnp.float32
    )


def right_dot(lhs_mat, rhs_mat):
    return lax.dot_general(
        lhs_mat, rhs_mat, (((1,), (1,)), ((), ())), preferred_element_type=jnp.float32
    )


def plain_dot(lhs_mat, rhs_mat):
    return jnp.dot(lhs_mat, rhs_mat, preferred_element_type=jnp.float32)


def attend_forward(queries, keys_all, values_all, live_keys):
    total_rows = queries.shape[0]
    row_block = min(512, total_rows)
    factor = HD ** (-0.5)
    key_heads = keys_all.reshape(total_rows, H, HD)
    value_heads = values_all.reshape(total_rows, H, HD)
    mixed_list = []
    stat_list = []
    for row_begin in range(0, total_rows, row_block):
        query_heads = queries[row_begin : row_begin + row_block].reshape(row_block, H, HD)
        scores = (
            jnp.einsum("qhd,khd->hqk", query_heads, key_heads, preferred_element_type=jnp.float32)
            * factor
        )
        scores = jnp.where(live_keys[None, None, :], scores, neg_big)
        row_max = jnp.max(scores, axis=-1, keepdims=True)
        exp_vals = jnp.exp(scores - row_max)
        row_total = jnp.sum(exp_vals, axis=-1, keepdims=True)
        prob_vals = (exp_vals / row_total).astype(jnp.bfloat16)
        mixed_rows = jnp.einsum(
            "hqk,khd->qhd", prob_vals, value_heads, preferred_element_type=jnp.float32
        )
        mixed_list.append(mixed_rows.reshape(row_block, H * HD))
        stat_list.append(row_max + jnp.log(row_total))
    return (jnp.concatenate(mixed_list, axis=0), jnp.concatenate(stat_list, axis=1))


def attend_backward(queries, keys_all, values_all, live_keys, log_totals, grad_mixed):
    total_rows = queries.shape[0]
    row_block = min(512, total_rows)
    factor = HD ** (-0.5)
    key_heads = keys_all.reshape(total_rows, H, HD)
    value_heads = values_all.reshape(total_rows, H, HD)
    grad_keys = jnp.zeros((total_rows, H, HD), jnp.float32)
    grad_values = jnp.zeros((total_rows, H, HD), jnp.float32)
    query_list = []
    for row_begin in range(0, total_rows, row_block):
        query_heads = queries[row_begin : row_begin + row_block].reshape(row_block, H, HD)
        grad_heads = grad_mixed[row_begin : row_begin + row_block].reshape(row_block, H, HD)
        scores = (
            jnp.einsum("qhd,khd->hqk", query_heads, key_heads, preferred_element_type=jnp.float32)
            * factor
        )
        scores = jnp.where(live_keys[None, None, :], scores, neg_big)
        prob_vals = jnp.exp(scores - log_totals[:, row_begin : row_begin + row_block])
        grad_probs = jnp.einsum(
            "qhd,khd->hqk", grad_heads, value_heads, preferred_element_type=jnp.float32
        )
        row_dot = jnp.sum(prob_vals * grad_probs, axis=-1, keepdims=True)
        grad_scores = (prob_vals * (grad_probs - row_dot)).astype(jnp.bfloat16)
        grad_query = (
            jnp.einsum("hqk,khd->qhd", grad_scores, key_heads, preferred_element_type=jnp.float32)
            * factor
        )
        query_list.append(grad_query.reshape(row_block, H * HD))
        grad_keys = (
            grad_keys
            + jnp.einsum(
                "hqk,qhd->khd", grad_scores, query_heads, preferred_element_type=jnp.float32
            )
            * factor
        )
        grad_values = grad_values + jnp.einsum(
            "hqk,qhd->khd",
            prob_vals.astype(jnp.bfloat16),
            grad_heads,
            preferred_element_type=jnp.float32,
        )
    return (
        jnp.concatenate(query_list, axis=0),
        grad_keys.reshape(total_rows, H * HD),
        grad_values.reshape(total_rows, H * HD),
    )


def shards(
    x_in,
    seq_units,
    deal,
    gain_attn,
    w_query,
    w_key,
    w_value,
    w_out,
    gain_ffn,
    w_gate,
    w_up,
    w_down,
    d_out,
):
    shard_count = lax.axis_size("shard")
    my_index = lax.axis_index("shard")
    width = x_in.shape[2]
    span = d_out.shape[2]
    unit_max = span // shard_count
    units_row = seq_units[0]
    order_row = deal[0]
    offsets = jnp.cumsum(units_row) - units_row
    inner_idx = jnp.arange(unit_max, dtype=jnp.int32)
    dest_idx = jnp.arange(shard_count, dtype=jnp.int32)
    counts = lookup(units_row, order_row)
    starts = lookup(offsets, order_row)
    row_index = starts[:, None] + jnp.minimum(inner_idx[None, :], counts[:, None] - 1)
    sent_live = inner_idx[None, :] < counts[:, None]
    local_rows = x_in[0]
    outgoing = jnp.where(
        sent_live[:, :, None], local_rows[row_index], jnp.zeros((), local_rows.dtype)
    )
    arrived = lax.all_to_all(outgoing, "shard", split_axis=0, concat_axis=0, tiled=True)
    own_count = jnp.sum(jnp.where(dest_idx == my_index, counts, 0))
    live_rows = jnp.broadcast_to(inner_idx[None, :] < own_count, (shard_count, unit_max)).reshape(
        span
    )
    wq_full, wk_full, wv_full, wo_full = (
        lax.all_gather(w_query, "shard", axis=0, tiled=True),
        lax.all_gather(w_key, "shard", axis=0, tiled=True),
        lax.all_gather(w_value, "shard", axis=0, tiled=True),
        lax.all_gather(w_out, "shard", axis=0, tiled=True),
    )
    tok_float = arrived.reshape(span, width).astype(jnp.float32)
    normed_one_f, norm_one_back = jax.vjp(rms_scale, tok_float, gain_attn)
    normed_one = normed_one_f.astype(jnp.bfloat16)
    queries = plain_dot(normed_one, wq_full).astype(jnp.bfloat16)
    keys_all = plain_dot(normed_one, wk_full).astype(jnp.bfloat16)
    values_all = plain_dot(normed_one, wv_full).astype(jnp.bfloat16)
    mixed_f, log_totals = attend_forward(queries, keys_all, values_all, live_rows)
    mixed_rows = mixed_f.astype(jnp.bfloat16)
    hidden_res = tok_float + plain_dot(mixed_rows, wo_full)
    wg_full, wu_full, wd_full = (
        lax.all_gather(w_gate, "shard", axis=0, tiled=True),
        lax.all_gather(w_up, "shard", axis=0, tiled=True),
        lax.all_gather(w_down, "shard", axis=0, tiled=True),
    )
    normed_two_f, norm_two_back = jax.vjp(rms_scale, hidden_res, gain_ffn)
    normed_two = normed_two_f.astype(jnp.bfloat16)
    gate_vals = plain_dot(normed_two, wg_full)
    up_vals = plain_dot(normed_two, wu_full)
    act_f, mix_back = jax.vjp(gelu_mix, gate_vals, up_vals)
    act_vals = act_f.astype(jnp.bfloat16)
    result = jnp.where(live_rows[:, None], hidden_res + plain_dot(act_vals, wd_full), 0.0)
    layer_out = result.astype(jnp.bfloat16).reshape(1, 1, span, width)
    wg_back, wu_back, wd_back = (
        lax.all_gather(w_gate, "shard", axis=0, tiled=True),
        lax.all_gather(w_up, "shard", axis=0, tiled=True),
        lax.all_gather(w_down, "shard", axis=0, tiled=True),
    )
    grad_y = jnp.where(live_rows[:, None], d_out[0, 0].astype(jnp.float32), 0.0)
    grad_ffn_b = grad_y.astype(jnp.bfloat16)
    grad_down = left_dot(act_vals, grad_ffn_b)
    grad_act = right_dot(grad_ffn_b, wd_back)
    grad_gate_f, grad_up_f = mix_back(grad_act)
    grad_gate_b = grad_gate_f.astype(jnp.bfloat16)
    grad_up_b = grad_up_f.astype(jnp.bfloat16)
    grad_wg = left_dot(normed_two, grad_gate_b)
    grad_wu = left_dot(normed_two, grad_up_b)
    grad_n2 = right_dot(grad_gate_b, wg_back) + right_dot(grad_up_b, wu_back)
    grad_h_norm, grad_gain_two = norm_two_back(grad_n2)
    ffn_share = (
        lax.psum_scatter(
            grad_wg.astype(jnp.bfloat16), "shard", scatter_dimension=0, tiled=True
        ).astype(jnp.float32),
        lax.psum_scatter(
            grad_wu.astype(jnp.bfloat16), "shard", scatter_dimension=0, tiled=True
        ).astype(jnp.float32),
        lax.psum_scatter(
            grad_down.astype(jnp.bfloat16), "shard", scatter_dimension=0, tiled=True
        ).astype(jnp.float32),
        lax.psum_scatter(
            grad_gain_two.astype(jnp.bfloat16), "shard", scatter_dimension=0, tiled=True
        ).astype(jnp.float32),
    )
    grad_hidden = grad_y + grad_h_norm
    wq_back, wk_back, wv_back, wo_back = (
        lax.all_gather(w_query, "shard", axis=0, tiled=True),
        lax.all_gather(w_key, "shard", axis=0, tiled=True),
        lax.all_gather(w_value, "shard", axis=0, tiled=True),
        lax.all_gather(w_out, "shard", axis=0, tiled=True),
    )
    grad_attn_b = grad_hidden.astype(jnp.bfloat16)
    grad_wo = left_dot(mixed_rows, grad_attn_b)
    grad_mixed = right_dot(grad_attn_b, wo_back).astype(jnp.bfloat16)
    grad_q_f, grad_k_f, grad_v_f = attend_backward(
        queries, keys_all, values_all, live_rows, log_totals, grad_mixed
    )
    grad_q_b = grad_q_f.astype(jnp.bfloat16)
    grad_k_b = grad_k_f.astype(jnp.bfloat16)
    grad_v_b = grad_v_f.astype(jnp.bfloat16)
    grad_wq = left_dot(normed_one, grad_q_b)
    grad_wk = left_dot(normed_one, grad_k_b)
    grad_wv = left_dot(normed_one, grad_v_b)
    grad_n1 = (
        right_dot(grad_q_b, wq_back) + right_dot(grad_k_b, wk_back) + right_dot(grad_v_b, wv_back)
    )
    grad_x_norm, grad_gain_one = norm_one_back(grad_n1)
    grad_tokens = (
        (grad_hidden + grad_x_norm).astype(jnp.bfloat16).reshape(shard_count, unit_max, width)
    )
    returned = lax.all_to_all(grad_tokens, "shard", split_axis=0, concat_axis=0, tiled=True)
    home_rows = (
        jnp.zeros(local_rows.shape, jnp.float32)
        .at[row_index]
        .add(jnp.where(sent_live[:, :, None], returned.astype(jnp.float32), 0.0))
    )
    grad_x = home_rows.astype(jnp.bfloat16)[None]
    attn_share = (
        lax.psum_scatter(
            grad_wq.astype(jnp.bfloat16), "shard", scatter_dimension=0, tiled=True
        ).astype(jnp.float32),
        lax.psum_scatter(
            grad_wk.astype(jnp.bfloat16), "shard", scatter_dimension=0, tiled=True
        ).astype(jnp.float32),
        lax.psum_scatter(
            grad_wv.astype(jnp.bfloat16), "shard", scatter_dimension=0, tiled=True
        ).astype(jnp.float32),
        lax.psum_scatter(
            grad_wo.astype(jnp.bfloat16), "shard", scatter_dimension=0, tiled=True
        ).astype(jnp.float32),
        lax.psum_scatter(
            grad_gain_one.astype(jnp.bfloat16), "shard", scatter_dimension=0, tiled=True
        ).astype(jnp.float32),
    )
    totals = (
        lax.psum(ffn_share[0].astype(jnp.bfloat16), "replica").astype(jnp.float32),
        lax.psum(ffn_share[1].astype(jnp.bfloat16), "replica").astype(jnp.float32),
        lax.psum(ffn_share[2].astype(jnp.bfloat16), "replica").astype(jnp.float32),
        lax.psum(ffn_share[3].astype(jnp.bfloat16), "replica").astype(jnp.float32),
        lax.psum(attn_share[0].astype(jnp.bfloat16), "replica").astype(jnp.float32),
        lax.psum(attn_share[1].astype(jnp.bfloat16), "replica").astype(jnp.float32),
        lax.psum(attn_share[2].astype(jnp.bfloat16), "replica").astype(jnp.float32),
        lax.psum(attn_share[3].astype(jnp.bfloat16), "replica").astype(jnp.float32),
        lax.psum(attn_share[4].astype(jnp.bfloat16), "replica").astype(jnp.float32),
    )
    return (
        layer_out,
        grad_x,
        totals[8],
        totals[3],
        totals[4],
        totals[5],
        totals[6],
        totals[7],
        totals[0],
        totals[1],
        totals[2],
    )


def solution(mesh):
    return jax.shard_map(
        shards,
        mesh=mesh,
        in_specs=(
            P("replica", "shard", None),
            P("replica", None),
            P("replica", None),
            P(),
            P("shard", None),
            P("shard", None),
            P("shard", None),
            P("shard", None),
            P(),
            P("shard", None),
            P("shard", None),
            P("shard", None),
            P("replica", "shard", None, None),
        ),
        out_specs=(
            P("replica", "shard", None, None),
            P("replica", "shard", None),
            P("shard"),
            P("shard"),
            P("shard", None),
            P("shard", None),
            P("shard", None),
            P("shard", None),
            P("shard", None),
            P("shard", None),
            P("shard", None),
        ),
        check_vma=False,
    )
```

profile of v0, /device:TPU:0, one launch (start us, length us, event | category | flops | bytes accessed | tf_op | source)
XLA Modules:
  0.0 894.3 jit_solution(441610172667195544)
XLA Ops:
  20.3 7.5 all-to-all-start
  29.4 35.4 %all-to-all-done = bf16[16,64,768]{2,1,0:T(8,128)(2,1)S(1)} async-done(((bf16[16,64,768]{2,1,0:T(8,128)(2,1)}), bf16[16,64,768]{2,1,0:T(8,128)(2,1)S(1)}, u32[]{:S(2)}, u32[]{:S(2)}) %all-to-all-start) | async-done | bytes 1572896 | tf_op jit(solution)/shard_map/all_to_all | solution.py:150
  70.1 33.1 %all-gather.12.cloned.1.call-done = bf16[768,768]{1,0:T(8,128)(2,1)} async-done(((bf16[48,768]{1,0:T(8,128)(2,1)}), bf16[768,768]{1,0:T(8,128)(2,1)}) %all-gather.12.cloned.1.call-update) | async-done | bytes 1179664 | tf_op jit(solution)/shard_map/all_gather | solution.py:157
  106.5 10.7 %fusion.65 = f32[12,512,1024]{2,1,0:T(8,128)} fusion(bf16[512,12,64]{0,2,1:T(8,128)(2,1)S(1)} %bitcast.124, bf16[1024,12,64]{0,2,1:T(8,128)(2,1)S(1)} %bitcast.120), kind=kOutput, calls=%fused_computation.130 | convolution fusion | flops 805306368 | bytes 27525120 | tf_op jit(solution)/shard_map/qhd,khd->hqk/dot_general | solution.py:53
  117.2 16.7 %fusion.12 = (f32[12,512]{1,0:T(8,128)S(1)}, f32[12,512]{1,0:T(8,128)S(1)}, f32[12,512,1024]{2,1,0:T(8,128)}) fusion(pred[1024]{0:T(1024)(128)(4,1)S(1)} %broadcast_in_dim.135, f32[12,512,1024]{2,1,0:T(8,128)} %fusion.65, bf16[512,12,64]{0,2,1:T(8,128)(2,1)S(1)} %bitcast.130, bf16[1024,12,64]{0,2,1:T(8,128)(2,1)} %bitcast.121), kind=kOutput, calls=%fused_computation.26 | convolution fusion | flops 843042816 | bytes 52741120 | tf_op jit(solution)/shard_map/qhd,khd->hqk/dot_general | solution.py:53
  133.9 18.7 %fusion = (f32[12,512]{1,0:T(8,128)S(1)}, f32[12,512]{1,0:T(8,128)S(1)}) fusion(f32[12,512]{1,0:T(8,128)S(1)} %get-tuple-element.19, f32[12,512,1024]{2,1,0:T(8,128)} %get-tuple-element.47, pred[1024]{0:T(1024)(128)(4,1)S(1)} %broadcast_in_dim.135, f32[12,512]{1,0:T(8,128)S(1)} %get-tuple-element.20, f32[12,512,1024]{2,1,0:T(8,128)} %fusion.65), kind=kLoop, calls=%fused_computation.14 | loop fusion | flops 50319360 | bytes 50430976 | tf_op jit(solution)/shard_map/reduce_sum | solution.py:59
  155.8 11.7 %fusion.37 = bf16[12,64,512]{2,1,0:T(8,128)(2,1)S(1)} fusion(bf16[1024,12,64]{0,2,1:T(8,128)(2,1)S(1)} %bitcast.126, f32[12,512]{1,0:T(8,128)S(1)} %get-tuple-element.17, f32[12,512]{1,0:T(8,128)S(1)} %get-tuple-element.19, f32[12,512,1024]{2,1,0:T(8,128)} %get-tuple-element.47, pred[1024]{0:T(1024)(128)(4,1)S(1)} %broadcast_in_dim.135), kind=kOutput, calls=%fused_computation.87 | convolution fusion | flops 837156864 | bytes 27575296 | tf_op jit(solution)/shard_map/hqk,khd->qhd/dot_general | solution.py:61
  167.6 12.2 %fusion.36 = bf16[12,64,512]{2,1,0:T(8,128)(2,1)} fusion(bf16[1024,12,64]{0,2,1:T(8,128)(2,1)S(1)} %bitcast.127, f32[12,512]{1,0:T(8,128)S(1)} %get-tuple-element.18, f32[12,512]{1,0:T(8,128)S(1)} %get-tuple-element.20, f32[12,512,1024]{2,1,0:T(8,128)} %fusion.65, pred[1024]{0:T(1024)(128)(4,1)S(1)} %broadcast_in_dim.135), kind=kOutput, calls=%fused_computation.86 | convolution fusion | flops 837156864 | bytes 27575296 | tf_op jit(solution)/shard_map/hqk,khd->qhd/dot_general | solution.py:61
  187.8 40.9 %all-gather.18.cloned.1.call-done = bf16[768,2048]{1,0:T(8,128)(2,1)} async-done(((bf16[48,2048]{1,0:T(8,128)(2,1)}), bf16[768,2048]{1,0:T(8,128)(2,1)}) %all-gather.18.cloned.1.call-update) | async-done | bytes 3145744 | tf_op jit(solution)/shard_map/all_gather | solution.py:172
  228.7 7.5 fusion.67
  236.1 38.5 %all-gather.16.cloned.1.call-done = bf16[768,2048]{1,0:T(8,128)(2,1)} async-done(((bf16[48,2048]{1,0:T(8,128)(2,1)}), bf16[768,2048]{1,0:T(8,128)(2,1)}) %all-gather.16.cloned.1.call-update) | async-done | bytes 3145744 | tf_op jit(solution)/shard_map/all_gather | solution.py:171
  274.7 9.0 %fusion.66 = f32[1024,2048]{1,0:T(8,128)} fusion(bf16[1024,768]{1,0:T(8,128)(2,1)} %copy-done.22, bf16[768,2048]{1,0:T(8,128)(2,1)} %all-gather.16.cloned.1.call-done), kind=kOutput, calls=%fused_computation.131 | convolution fusion | flops 3221225472 | bytes 13107200 | tf_op jit(solution)/shard_map/dot_general | solution.py:39
  283.7 37.1 %all-gather.20.cloned.1.call-done = bf16[2048,768]{1,0:T(8,128)(2,1)} async-done(((bf16[128,768]{1,0:T(8,128)(2,1)}), bf16[2048,768]{1,0:T(8,128)(2,1)}) %all-gather.20.cloned.1.call-update) | async-done | bytes 3145744 | tf_op jit(solution)/shard_map/all_gather | solution.py:173
  320.8 15.1 %multiply_convert_fusion.2 = (bf16[1024,2048]{1,0:T(8,128)(2,1)S(1)}, bf16[1024,2048]{1,0:T(8,128)(2,1)}, bf16[1024,2048]{1,0:T(8,128)(2,1)}) fusion(f32[1024,2048]{1,0:T(8,128)} %fusion.66, f32[1024,2048]{1,0:T(8,128)} %fusion.67, bf16[2048,768]{1,0:T(8,128)(2,1)} %all-gather.20.cloned.1.call-done, bf16[1,1,1024,768]{3,2,1,0:T(8,128)(2,1)S(1)} %copy-done.16, ...), kind=kOutput, calls=%fused_computation.35 | convolution fusion | flops 3278110720 | bytes 34079744 | tf_op jit(solution)/shard_map/dot_general | solution.py:33
  335.9 7.3 fusion.68
  358.1 10.8 %fusion.69 = f32[12,512,1024]{2,1,0:T(8,128)} fusion(bf16[512,12,64]{0,2,1:T(8,128)(2,1)S(1)} %bitcast.132, bf16[1024,12,64]{0,2,1:T(8,128)(2,1)S(1)} %bitcast.128), kind=kOutput, calls=%fused_computation.134 | convolution fusion | flops 805306368 | bytes 27525120 | tf_op jit(solution)/shard_map/qhd,khd->hqk/dot_general | solution.py:87
  368.9 12.6 %fusion.4 = f32[12,64,1024]{2,1,0:T(8,128)} fusion(bf16[512,12,64]{0,2,1:T(8,128)(2,1)S(1)} %bitcast.133, f32[12,512]{1,0:T(8,128)S(1)} %get-tuple-element.53, f32[12,512,1024]{2,1,0:T(8,128)} %fusion.65, pred[1024]{0:T(1024)(128)(4,1)S(1)} %broadcast_in_dim.135), kind=kOutput, calls=%fused_computation.18 | convolution fusion | flops 830472192 | bytes 29123584 | tf_op jit(solution)/shard_map/hqk,qhd->khd/dot_general | solution.py:104
  381.5 35.6 %multiply_reduce_fusion.1 = (f32[12,512]{1,0:T(8,128)S(1)}, f32[12,512]{1,0:T(8,128)S(1)}, f32[12,512,1024]{2,1,0:T(8,128)}) fusion(f32[12,512]{1,0:T(8,128)S(1)} %get-tuple-element.54, f32[12,512,1024]{2,1,0:T(8,128)} %get-tuple-element.47, pred[1024]{0:T(1024)(128)(4,1)S(1)} %broadcast_in_dim.135, f32[12,512,1024]{2,1,0:T(8,128)} %fusion.69, ...), kind=kOutput, calls=%fused_computation.6 | convolution fusion | flops 868208640 | bytes 103121920 | tf_op jit(solution)/shard_map/qhd,khd->hqk/dot_general | solution.py:87
  417.1 12.3 %add_convert_fusion = bf16[12,64,1024]{2,1,0:T(8,128)(2,1)S(1)} fusion(f32[12,64,1024]{2,1,0:T(8,128)} %fusion.4, bf16[512,12,64]{0,2,1:T(8,128)(2,1)S(1)} %bitcast.138, f32[12,512]{1,0:T(8,128)S(1)} %get-tuple-element.54, f32[12,512,1024]{2,1,0:T(8,128)} %get-tuple-element.47, pred[1024]{0:T(1024)(128)(4,1)S(1)} %broadcast_in_dim.135), kind=kOutput, calls=%fused_computation.64 | convolution fusion | flops 832045056 | bytes 30696448 | tf_op jit(solution)/shard_map/hqk,qhd->khd/dot_general | solution.py:104
  433.1 42.5 %multiply_convert_fusion.1 = (bf16[12,512,1024]{2,1,0:T(8,128)(2,1)}, bf16[12,512,1024]{2,1,0:T(8,128)(2,1)}) fusion(f32[12,512,1024]{2,1,0:T(8,128)} %get-tuple-element.51, f32[12,512]{1,0:T(8,128)S(1)} %get-tuple-element.15, f32[12,512]{1,0:T(8,128)S(1)} %get-tuple-element.54, f32[12,512,1024]{2,1,0:T(8,128)} %get-tuple-element.47, ...), kind=kLoop, calls=%fused_computation.5 | loop fusion | flops 75497472 | bytes 125928448 | tf_op jit(solution)/shard_map/convert_element_type | solution.py:91
  475.7 8.6 multiply_convert_fusion.7
  484.3 8.7 multiply_convert_fusion.6
  512.5 7.9 convolution_convert_fusion
  520.5 7.9 convolution_convert_fusion.2
  528.8 7.8 convolution_convert_fusion.1
  552.7 60.4 %reduce-scatter.10.cloned.1.call-done = bf16[48,768]{1,0:T(8,128)(2,1)} async-done(((bf16[768,768]{1,0:T(8,128)(2,1)}), bf16[48,768]{1,0:T(8,128)(2,1)}) %reduce-scatter.10.cloned.1.call-update) | async-done | bytes 73744 | tf_op jit(solution)/shard_map/reduce_scatter | solution.py:250
  613.1 69.0 %reduce-scatter.20.cloned.1.call-done = bf16[128,768]{1,0:T(8,128)(2,1)} async-done(((bf16[2048,768]{1,0:T(8,128)(2,1)}), bf16[128,768]{1,0:T(8,128)(2,1)}) %reduce-scatter.20.cloned.1.call-update) | async-done | bytes 196624 | tf_op jit(solution)/shard_map/reduce_scatter | solution.py:206
  682.2 69.1 %reduce-scatter.16.cloned.1.call-done = bf16[48,2048]{1,0:T(8,128)(2,1)} async-done(((bf16[768,2048]{1,0:T(8,128)(2,1)}), bf16[48,2048]{1,0:T(8,128)(2,1)}) %reduce-scatter.16.cloned.1.call-update) | async-done | bytes 196624 | tf_op jit(solution)/shard_map/reduce_scatter | solution.py:200
  751.3 69.1 %reduce-scatter.18.cloned.1.call-done = bf16[48,2048]{1,0:T(8,128)(2,1)} async-done(((bf16[768,2048]{1,0:T(8,128)(2,1)}), bf16[48,2048]{1,0:T(8,128)(2,1)}) %reduce-scatter.18.cloned.1.call-update) | async-done | bytes 196624 | tf_op jit(solution)/shard_map/reduce_scatter | solution.py:203
  820.5 8.6 fusion.35
  829.1 29.5 %all-reduce.2 = (bf16[768]{0:T(1024)(128)(2,1)S(1)}, bf16[768]{0:T(1024)(128)(2,1)S(1)}) all-reduce(bf16[768]{0:T(1024)(128)(2,1)S(1)} %get-tuple-element.13, bf16[768]{0:T(1024)(128)(2,1)S(1)} %copy-done.36), channel_id=2, replica_groups=mesh['shard'=16,'replica'=2] {'shard'}, use_global_device_ids=true, to_apply=%region_16.17.clone | all-reduce | flops 1536 | bytes 6144
  866.7 8.6 scatter_custom_fusion
  (185 shorter events, 108.5 us)
Async XLA Ops:
  7.2 59.6 %all-gather.10.cloned.1.call-start = ((), (), s32[]{:S(2)}) async-start(), calls=%async_computation.10 | async-start | bytes 1253376 | tf_op jit(solution)/shard_map/all_gather | solution.py:156
  7.9 95.3 %all-gather.12.cloned.1.call-start = ((), (), s32[]{:S(2)}) async-start(), calls=%async_computation.11 | async-start | bytes 1253376 | tf_op jit(solution)/shard_map/all_gather | solution.py:157
  8.7 143.9 %all-gather.8.cloned.1.call-start = ((), (), s32[]{:S(2)}) async-start(), calls=%async_computation.9 | async-start | bytes 1253376 | tf_op jit(solution)/shard_map/all_gather | solution.py:158
  9.4 172.7 %all-gather.14.cloned.1.call-start = ((), (), s32[]{:S(2)}) async-start(), calls=%async_computation.12 | async-start | bytes 1253376 | tf_op jit(solution)/shard_map/all_gather | solution.py:159
  10.0 218.7 %all-gather.18.cloned.1.call-start = ((), (), s32[]{:S(2)}) async-start(), calls=%async_computation.14 | async-start | bytes 3342336 | tf_op jit(solution)/shard_map/all_gather | solution.py:172
  10.6 264.1 %all-gather.16.cloned.1.call-start = ((), (), s32[]{:S(2)}) async-start(), calls=%async_computation.13 | async-start | bytes 3342336 | tf_op jit(solution)/shard_map/all_gather | solution.py:171
  20.3 44.9 %copy-start.26 = (f32[768]{0:T(1024)S(1)}, f32[768]{0:T(1024)}, u32[]{:S(2)}) copy-start(f32[768]{0:T(1024)} %param.16) | copy-start | bytes 9220
  20.3 44.4 %all-to-all-start = ((bf16[16,64,768]{2,1,0:T(8,128)(2,1)}), bf16[16,64,768]{2,1,0:T(8,128)(2,1)S(1)}, u32[]{:S(2)}, u32[]{:S(2)}) async-start(bf16[16,64,768]{2,1,0:T(8,128)(2,1)} %broadcast_select_fusion), calls=%async_computation | async-start | bytes 3145728 | tf_op jit(solution)/shard_map/all_to_all | solution.py:150
  27.9 292.9 %all-gather.20.cloned.1.call-start = ((), (), s32[]{:S(2)}) async-start(), calls=%async_computation.15 | async-start | bytes 3342336 | tf_op jit(solution)/shard_map/all_gather | solution.py:173
  28.6 524.1 %reduce-scatter.14.cloned.1.call-start = ((), (), s32[]{:S(2)}) async-start(), calls=%async_computation.19 | async-start | bytes 1253376 | tf_op jit(solution)/shard_map/reduce_scatter | solution.py:256
  64.8 120.6 %copy-start.2 = (bf16[16,64,768]{2,1,0:T(8,128)(2,1)}, bf16[16,64,768]{2,1,0:T(8,128)(2,1)S(1)}, u32[]{:S(2)}) copy-start(bf16[16,64,768]{2,1,0:T(8,128)(2,1)S(1)} %all-to-all-done) | copy-start | bytes 4718596
  70.1 36.3 %copy-start.6 = (bf16[512,768]{0,1:T(8,128)(2,1)}, bf16[512,768]{0,1:T(8,128)(2,1)S(1)}, u32[]{:S(2)}) copy-start(bf16[512,768]{0,1:T(8,128)(2,1)S(1)} %get-tuple-element.39) | copy-start | bytes 2359300
  70.1 47.1 %copy-start.14 = (bf16[512,768]{0,1:T(8,128)(2,1)}, bf16[512,768]{0,1:T(8,128)(2,1)S(1)}, u32[]{:S(2)}) copy-start(bf16[512,768]{0,1:T(8,128)(2,1)S(1)} %get-tuple-element.40) | copy-start | bytes 2359300
  106.5 10.8 %copy-start.4 = (bf16[1024,768]{0,1:T(8,128)(2,1)}, bf16[1024,768]{0,1:T(8,128)(2,1)S(1)}, u32[]{:S(2)}) copy-start(bf16[1024,768]{0,1:T(8,128)(2,1)S(1)} %convolution_convert_fusion.4) | copy-start | bytes 4718596
  155.8 11.7 %copy-start.8 = (bf16[1024,768]{0,1:T(8,128)(2,1)}, bf16[1024,768]{0,1:T(8,128)(2,1)S(1)}, u32[]{:S(2)}) copy-start(bf16[1024,768]{0,1:T(8,128)(2,1)S(1)} %convolution_convert_fusion.6) | copy-start | bytes 4718596
  187.8 40.9 %copy-start.22 = (bf16[1024,768]{1,0:T(8,128)(2,1)}, bf16[1024,768]{1,0:T(8,128)(2,1)S(1)}, u32[]{:S(2)}) copy-start(bf16[1024,768]{1,0:T(8,128)(2,1)S(1)} %multiply_convert_fusion.5) | copy-start | bytes 4718596
  236.1 84.7 %copy-start.16 = (bf16[1,1,1024,768]{3,2,1,0:T(8,128)(2,1)S(1)}, bf16[1,1,1024,768]{3,2,1,0:T(8,128)(2,1)}, u32[]{:S(2)}) copy-start(bf16[1,1,1024,768]{3,2,1,0:T(8,128)(2,1)} %param.25) | copy-start | bytes 4718596
  320.8 15.1 %copy-start.38 = (bf16[768,2048]{1,0:T(8,128)(2,1)S(1)}, bf16[768,2048]{1,0:T(8,128)(2,1)}, u32[]{:S(2)}) copy-start(bf16[768,2048]{1,0:T(8,128)(2,1)} %all-gather.16.cloned.1.call-done) | copy-start | bytes 9437188
  353.3 199.4 %reduce-scatter.12.cloned.1.call-start = ((), (), s32[]{:S(2)}) async-start(), calls=%async_computation.18 | async-start | bytes 1253376 | tf_op jit(solution)/shard_map/reduce_scatter | solution.py:253
  417.1 13.5 %copy-start.20 = (bf16[16,64,768]{2,1,0:T(8,128)(2,1)S(1)}, bf16[16,64,768]{2,1,0:T(8,128)(2,1)}, u32[]{:S(2)}) copy-start(bf16[16,64,768]{2,1,0:T(8,128)(2,1)} %fusion.31) | copy-start | bytes 4718596
  433.1 119.6 %reduce-scatter.8.cloned.1.call-start = ((), (), s32[]{:S(2)}) async-start(), calls=%async_computation.16 | async-start | bytes 1253376 | tf_op jit(solution)/shard_map/reduce_scatter | solution.py:247
  433.1 42.6 %copy-start.5 = (bf16[1024,768]{0,1:T(8,128)(2,1)S(1)}, bf16[1024,768]{0,1:T(8,128)(2,1)}, u32[]{:S(2)}) copy-start(bf16[1024,768]{0,1:T(8,128)(2,1)} %copy-done.4) | copy-start | bytes 4718596
  484.3 8.7 copy-start.19
  495.4 117.7 %reduce-scatter.10.cloned.1.call-start = ((), (), s32[]{:S(2)}) async-start(), calls=%async_computation.17 | async-start | bytes 1253376 | tf_op jit(solution)/shard_map/reduce_scatter | solution.py:250
  512.4 169.8 %reduce-scatter.20.cloned.1.call-start = ((), (), s32[]{:S(2)}) async-start(), calls=%async_computation.22 | async-start | bytes 3342336 | tf_op jit(solution)/shard_map/reduce_scatter | solution.py:206
  520.4 230.9 %reduce-scatter.16.cloned.1.call-start = ((), (), s32[]{:S(2)}) async-start(), calls=%async_computation.20 | async-start | bytes 3342336 | tf_op jit(solution)/shard_map/reduce_scatter | solution.py:200
  528.4 292.1 %reduce-scatter.18.cloned.1.call-start = ((), (), s32[]{:S(2)}) async-start(), calls=%async_computation.21 | async-start | bytes 3342336 | tf_op jit(solution)/shard_map/reduce_scatter | solution.py:203
  547.3 317.4 %all-to-all-start.1 = ((bf16[16,64,768]{2,1,0:T(8,128)(2,1)}), bf16[16,64,768]{2,1,0:T(8,128)(2,1)S(1)}, u32[]{:S(2)}, u32[]{:S(2)}) async-start(bf16[16,64,768]{2,1,0:T(8,128)(2,1)} %bitcast.26), calls=%async_computation.1 | async-start | bytes 3145728 | tf_op jit(solution)/shard_map/all_to_all | solution.py:239
  551.2 325.1 %all-reduce.7.cloned.1.call-start = ((), (), s32[]{:S(2)}) async-start(), calls=%async_computation.23 | async-start | bytes 1769472 | tf_op jit(solution)/shard_map/psum | solution.py:268
  820.5 8.6 copy-start.36
  820.5 44.2 %copy-start.33 = (pred[16,64]{1,0:T(8,128)(4,1)S(1)}, pred[16,64]{1,0:T(8,128)(4,1)}, u32[]{:S(2)}) copy-start(pred[16,64]{1,0:T(8,128)(4,1)} %copy-done.32) | copy-start | bytes 3076
  866.7 20.9 %copy-start.1 = (bf16[1,512,768]{2,1,0:T(8,128)(2,1)S(1)}, bf16[1,512,768]{2,1,0:T(8,128)(2,1)}, u32[]{:S(2)}) copy-start(bf16[1,512,768]{2,1,0:T(8,128)(2,1)} %param.13) | copy-start | bytes 2359300
  (29 other events, 91.8 us)
Sparse Core Ops, SparseCore 0:
  10.3 51.5 all-gather.9
  64.1 39.0 all-gather.11
  105.6 37.1 all-gather.7
  144.9 37.1 all-gather.13
  184.2 44.3 all-gather.17
  230.8 43.8 all-gather.15
  276.9 43.8 all-gather.19
  353.5 56.5 reduce-scatter.13
  433.2 56.6 reduce-scatter.11
  495.5 56.5 reduce-scatter.7
  555.8 57.3 reduce-scatter.9
  616.8 65.3 reduce-scatter.19
  686.0 65.2 reduce-scatter.15
  755.0 65.4 reduce-scatter.17
  823.0 35.4 all-reduce.6
where the time goes:
time: 900 us; the launch traced here: 894 us
  waiting for transfers between devices  460 us (51%)
  matrix products  262 us (29%)
  other arithmetic  97.7 us (11%)
  blocking collectives  34.4 us (4%)
  between operations  15.4 us (2%)
  starting transfers between devices  12.7 us (1%)
  local copies, waits for them, and re-layouts  12.1 us (1%)
    reduce_scatter x1, waiting for transfers between devices, shards(): lax.psum_scatter(grad_wg.astype(jnp.bfloat16), 'shard', scatter_dimension...  69.1 us
    reduce_scatter x1, waiting for transfers between devices, shards(): lax.psum_scatter(grad_wu.astype(jnp.bfloat16), 'shard', scatter_dimension...  69.1 us
    reduce_scatter x1, waiting for transfers between devices, shards(): lax.psum_scatter(grad_down.astype(jnp.bfloat16), 'shard', scatter_dimensi...  69 us
    reduce_scatter x1, waiting for transfers between devices, shards(): lax.psum_scatter(grad_wk.astype(jnp.bfloat16), 'shard', scatter_dimension...  60.4 us
    dot_general x2, matrix products, attend_backward(): jnp.einsum('qhd,khd->hqk', grad_heads, value_heads, preferred_element_typ...  46.4 us
    convert_element_type x1, other arithmetic, attend_backward(): grad_scores = (prob_vals * (grad_probs - row_dot)).astype(jnp.bfloat16)  42.5 us
    all_gather x1, waiting for transfers between devices, shards(): lax.all_gather(w_up, 'shard', axis=0, tiled=True)  40.9 us
    all_gather x1, waiting for transfers between devices, shards(): lax.all_gather(w_gate, 'shard', axis=0, tiled=True)  38.5 us
  transfers between devices with their start and end apart: 17, of which 10 were waited for; matrix products, arithmetic and copies ran while one was open for 36% of the time, Pallas kernels for 0%

commit v1 on v0

--- a/solution.py
+++ b/solution.py
@@ -7,6 +7,18 @@
 HD = 64
 norm_eps = 1e-06
 neg_big = -1e30
+
+
+def collect(x, axis, dim):
+    ways, here, step = (lax.axis_size(axis), lax.axis_index(axis), x.shape[dim])
+    line, have = (x, 1)
+    while have < ways:
+        line = jnp.concatenate(
+            [line, lax.ppermute(line, axis, [(d, (d - have) % ways) for d in range(ways)])],
+            axis=dim,
+        )
+        have = 2 * have
+    return jnp.roll(line, here * step, axis=dim)
 
 
 def rms_scale(tok_rows, gain_vec):
@@ -170,7 +182,7 @@
     wg_full, wu_full, wd_full = (
         lax.all_gather(w_gate, "shard", axis=0, tiled=True),
         lax.all_gather(w_up, "shard", axis=0, tiled=True),
-        lax.all_gather(w_down, "shard", axis=0, tiled=True),
+        collect(w_down, "shard", 0),
     )
     normed_two_f, norm_two_back = jax.vjp(rms_scale, hidden_res, gain_ffn)
     normed_two = normed_two_f.astype(jnp.bfloat16)

time: 900 us -> 954 us (1.060)
  waiting for transfers between devices: 460 us -> 493 us
  local copies, waits for them, and re-layouts: 12.1 us -> 24 us
    ppermute x0 -> x4, waiting for transfers between devices: none -> 101 us  [collect(): lax.ppermute(line, axis, [(d, (d - have) % ways) for d in range(ways)])]
    reduce_scatter x1, waiting for transfers between devices: 60.4 us -> 0.01 us  [shards(): lax.psum_scatter(grad_wk.astype(jnp.bfloat16), 'shard', scatter_dimension...]
    unnamed x91 -> x110, local copies, waits for them, and re-layouts: 7.63 us -> 18.2 us
  transfers between devices with their start and end apart: 17 -> 21, of which waited for: 10 -> 13; matrix products, arithmetic and copies ran while one was open for 36% -> 35% of each run, Pallas kernels for 0% -> 0%
where the time goes in v1:
time: 954 us; the launch traced here: 949 us
  waiting for transfers between devices  493 us (52%)
  matrix products  261 us (27%)
  other arithmetic  101 us (11%)
  blocking collectives  34.7 us (4%)
  local copies, waits for them, and re-layouts  24 us (3%)
  starting transfers between devices  19.4 us (2%)
  between operations  15.7 us (2%)
    ppermute x4, waiting for transfers between devices, collect(): lax.ppermute(line, axis, [(d, (d - have) % ways) for d in range(ways)])  101 us
    reduce_scatter x1, waiting for transfers between devices, shards(): lax.psum_scatter(grad_wg.astype(jnp.bfloat16), 'shard', scatter_dimension...  69.1 us
    reduce_scatter x1, waiting for transfers between devices, shards(): lax.psum_scatter(grad_wu.astype(jnp.bfloat16), 'shard', scatter_dimension...  69 us
    reduce_scatter x1, waiting for transfers between devices, shards(): lax.psum_scatter(grad_down.astype(jnp.bfloat16), 'shard', scatter_dimensi...  62.3 us
    dot_general x2, matrix products, attend_backward(): jnp.einsum('qhd,khd->hqk', grad_heads, value_heads, preferred_element_typ...  46.4 us
    convert_element_type x1, other arithmetic, attend_backward(): grad_scores = (prob_vals * (grad_probs - row_dot)).astype(jnp.bfloat16)  42.5 us
    all_gather x1, waiting for transfers between devices, shards(): lax.all_gather(w_up, 'shard', axis=0, tiled=True)  40.9 us
    all_gather x1, waiting for transfers between devices, shards(): lax.all_gather(w_gate, 'shard', axis=0, tiled=True)  38.5 us
  transfers between devices with their start and end apart: 21, of which 13 were waited for; matrix products, arithmetic and copies ran while one was open for 35% of the time, Pallas kernels for 0%

profile of v1, /device:TPU:0, one launch (start us, length us, event | category | flops | bytes accessed | tf_op | source)
XLA Modules:
  0.0 949.2 jit_solution(3864429193989277587)
XLA Ops:
  20.3 7.5 all-to-all-start
  29.4 35.4 %all-to-all-done = bf16[16,64,768]{2,1,0:T(8,128)(2,1)S(1)} async-done(((bf16[16,64,768]{2,1,0:T(8,128)(2,1)}), bf16[16,64,768]{2,1,0:T(8,128)(2,1)S(1)}, u32[]{:S(2)}, u32[]{:S(2)}) %all-to-all-start) | async-done | bytes 1572896 | tf_op jit(solution)/shard_map/all_to_all | solution.py:162
  70.1 33.1 %all-gather.12.cloned.1.call-done = bf16[768,768]{1,0:T(8,128)(2,1)} async-done(((bf16[48,768]{1,0:T(8,128)(2,1)}), bf16[768,768]{1,0:T(8,128)(2,1)}) %all-gather.12.cloned.1.call-update) | async-done | bytes 1179664 | tf_op jit(solution)/shard_map/all_gather | solution.py:169
  106.5 10.7 %fusion.70 = f32[12,512,1024]{2,1,0:T(8,128)} fusion(bf16[512,12,64]{0,2,1:T(8,128)(2,1)S(1)} %bitcast.123, bf16[1024,12,64]{0,2,1:T(8,128)(2,1)S(1)} %bitcast.119), kind=kOutput, calls=%fused_computation.146 | convolution fusion | flops 805306368 | bytes 27525120 | tf_op jit(solution)/shard_map/qhd,khd->hqk/dot_general | solution.py:65
  117.2 16.7 %fusion.12 = (f32[12,512]{1,0:T(8,128)S(1)}, f32[12,512]{1,0:T(8,128)S(1)}, f32[12,512,1024]{2,1,0:T(8,128)}) fusion(pred[1024]{0:T(1024)(128)(4,1)S(1)} %broadcast_in_dim.135, f32[12,512,1024]{2,1,0:T(8,128)} %fusion.70, bf16[512,12,64]{0,2,1:T(8,128)(2,1)S(1)} %bitcast.129, bf16[1024,12,64]{0,2,1:T(8,128)(2,1)} %bitcast.120), kind=kOutput, calls=%fused_computation.26 | convolution fusion | flops 843042816 | bytes 52741120 | tf_op jit(solution)/shard_map/qhd,khd->hqk/dot_general | solution.py:65
  133.9 18.7 %fusion = (f32[12,512]{1,0:T(8,128)S(1)}, f32[12,512]{1,0:T(8,128)S(1)}) fusion(f32[12,512]{1,0:T(8,128)S(1)} %get-tuple-element.19, f32[12,512,1024]{2,1,0:T(8,128)} %get-tuple-element.47, pred[1024]{0:T(1024)(128)(4,1)S(1)} %broadcast_in_dim.135, f32[12,512]{1,0:T(8,128)S(1)} %get-tuple-element.20, f32[12,512,1024]{2,1,0:T(8,128)} %fusion.70), kind=kLoop, calls=%fused_computation.14 | loop fusion | flops 50319360 | bytes 50430976 | tf_op jit(solution)/shard_map/reduce_sum | solution.py:71
  155.8 11.7 %fusion.39 = bf16[12,64,512]{2,1,0:T(8,128)(2,1)S(1)} fusion(bf16[1024,12,64]{0,2,1:T(8,128)(2,1)S(1)} %bitcast.125, f32[12,512]{1,0:T(8,128)S(1)} %get-tuple-element.17, f32[12,512]{1,0:T(8,128)S(1)} %get-tuple-element.19, f32[12,512,1024]{2,1,0:T(8,128)} %get-tuple-element.47, pred[1024]{0:T(1024)(128)(4,1)S(1)} %broadcast_in_dim.135), kind=kOutput, calls=%fused_computation.90 | convolution fusion | flops 837156864 | bytes 27575296 | tf_op jit(solution)/shard_map/hqk,khd->qhd/dot_general | solution.py:73
  167.5 12.2 %fusion.38 = bf16[12,64,512]{2,1,0:T(8,128)(2,1)} fusion(bf16[1024,12,64]{0,2,1:T(8,128)(2,1)S(1)} %bitcast.126, f32[12,512]{1,0:T(8,128)S(1)} %get-tuple-element.18, f32[12,512]{1,0:T(8,128)S(1)} %get-tuple-element.20, f32[12,512,1024]{2,1,0:T(8,128)} %fusion.70, pred[1024]{0:T(1024)(128)(4,1)S(1)} %broadcast_in_dim.135), kind=kOutput, calls=%fused_computation.89 | convolution fusion | flops 837156864 | bytes 27575296 | tf_op jit(solution)/shard_map/hqk,khd->qhd/dot_general | solution.py:73
  187.8 40.9 %all-gather.18.cloned.1.call-done = bf16[768,2048]{1,0:T(8,128)(2,1)} async-done(((bf16[48,2048]{1,0:T(8,128)(2,1)}), bf16[768,2048]{1,0:T(8,128)(2,1)}) %all-gather.18.cloned.1.call-update) | async-done | bytes 3145744 | tf_op jit(solution)/shard_map/all_gather | solution.py:184
  228.7 7.5 fusion.72
  236.1 38.5 %all-gather.16.cloned.1.call-done = bf16[768,2048]{1,0:T(8,128)(2,1)} async-done(((bf16[48,2048]{1,0:T(8,128)(2,1)}), bf16[768,2048]{1,0:T(8,128)(2,1)}) %all-gather.16.cloned.1.call-update) | async-done | bytes 3145744 | tf_op jit(solution)/shard_map/all_gather | solution.py:183
  274.6 9.0 fusion.71
  283.7 37.1 %all-gather.20.cloned.1.call-done = bf16[2048,768]{1,0:T(8,128)(2,1)} async-done(((bf16[128,768]{1,0:T(8,128)(2,1)}), bf16[2048,768]{1,0:T(8,128)(2,1)}) %all-gather.20.cloned.1.call-update) | async-done | bytes 3145744 | tf_op jit(solution)/shard_map/all_gather | solution.py:198
  320.8 15.1 %multiply_convert_fusion.2 = (bf16[1024,2048]{1,0:T(8,128)(2,1)S(1)}, bf16[1024,2048]{1,0:T(8,128)(2,1)}, bf16[1024,2048]{1,0:T(8,128)(2,1)}) fusion(f32[1024,2048]{1,0:T(8,128)} %fusion.71, f32[1024,2048]{1,0:T(8,128)} %fusion.72, bf16[2048,768]{1,0:T(8,128)(2,1)} %all-gather.20.cloned.1.call-done, bf16[1,1,1024,768]{3,2,1,0:T(8,128)(2,1)S(1)} %copy-done.19, ...), kind=kOutput, calls=%fused_computation.35 | convolution fusion | flops 3278110720 | bytes 34079744 | tf_op jit(solution)/shard_map/dot_general | solution.py:45
  335.9 7.3 fusion.73
  358.1 10.8 %fusion.74 = f32[12,512,1024]{2,1,0:T(8,128)} fusion(bf16[512,12,64]{0,2,1:T(8,128)(2,1)S(1)} %bitcast.131, bf16[1024,12,64]{0,2,1:T(8,128)(2,1)S(1)} %bitcast.127), kind=kOutput, calls=%fused_computation.150 | convolution fusion | flops 805306368 | bytes 27525120 | tf_op jit(solution)/shard_map/qhd,khd->hqk/dot_general | solution.py:99
  368.9 12.6 %fusion.4 = f32[12,64,1024]{2,1,0:T(8,128)} fusion(bf16[512,12,64]{0,2,1:T(8,128)(2,1)S(1)} %bitcast.132, f32[12,512]{1,0:T(8,128)S(1)} %get-tuple-element.53, f32[12,512,1024]{2,1,0:T(8,128)} %fusion.70, pred[1024]{0:T(1024)(128)(4,1)S(1)} %broadcast_in_dim.135), kind=kOutput, calls=%fused_computation.18 | convolution fusion | flops 830472192 | bytes 29123584 | tf_op jit(solution)/shard_map/hqk,qhd->khd/dot_general | solution.py:116
  381.5 35.6 %multiply_reduce_fusion.1 = (f32[12,512]{1,0:T(8,128)S(1)}, f32[12,512]{1,0:T(8,128)S(1)}, f32[12,512,1024]{2,1,0:T(8,128)}) fusion(f32[12,512]{1,0:T(8,128)S(1)} %get-tuple-element.54, f32[12,512,1024]{2,1,0:T(8,128)} %get-tuple-element.47, pred[1024]{0:T(1024)(128)(4,1)S(1)} %broadcast_in_dim.135, f32[12,512,1024]{2,1,0:T(8,128)} %fusion.74, ...), kind=kOutput, calls=%fused_computation.6 | convolution fusion | flops 868208640 | bytes 103121920 | tf_op jit(solution)/shard_map/qhd,khd->hqk/dot_general | solution.py:99
  417.1 12.3 %add_convert_fusion = bf16[12,64,1024]{2,1,0:T(8,128)(2,1)S(1)} fusion(f32[12,64,1024]{2,1,0:T(8,128)} %fusion.4, bf16[512,12,64]{0,2,1:T(8,128)(2,1)S(1)} %bitcast.137, f32[12,512]{1,0:T(8,128)S(1)} %get-tuple-element.54, f32[12,512,1024]{2,1,0:T(8,128)} %get-tuple-element.47, pred[1024]{0:T(1024)(128)(4,1)S(1)} %broadcast_in_dim.135), kind=kOutput, calls=%fused_computation.64 | convolution fusion | flops 832045056 | bytes 30696448 | tf_op jit(solution)/shard_map/hqk,qhd->khd/dot_general | solution.py:116
  433.0 42.5 %multiply_convert_fusion.1 = (bf16[12,512,1024]{2,1,0:T(8,128)(2,1)}, bf16[12,512,1024]{2,1,0:T(8,128)(2,1)}) fusion(f32[12,512,1024]{2,1,0:T(8,128)} %get-tuple-element.51, f32[12,512]{1,0:T(8,128)S(1)} %get-tuple-element.15, f32[12,512]{1,0:T(8,128)S(1)} %get-tuple-element.54, f32[12,512,1024]{2,1,0:T(8,128)} %get-tuple-element.47, ...), kind=kLoop, calls=%fused_computation.5 | loop fusion | flops 75497472 | bytes 125928448 | tf_op jit(solution)/shard_map/convert_element_type | solution.py:103
  475.6 8.6 multiply_convert_fusion.7
  484.2 8.9 multiply_convert_fusion.6
  514.6 7.5 convolution_convert_fusion
  537.9 10.9 %collective-permute-done.1 = bf16[256,768]{1,0:T(8,128)(2,1)S(1)} collective-permute-done((bf16[256,768]{1,0:T(8,128)(2,1)S(1)}, bf16[256,768]{1,0:T(8,128)(2,1)S(1)}, u32[]{:S(2)}, u32[]{:S(2)}) %collective-permute-start.1) | collective-permute-done | bytes 393248 | tf_op jit(solution)/shard_map/ppermute | solution.py:17
  557.9 12.7 %collective-permute-done.2 = bf16[512,768]{1,0:T(8,128)(2,1)S(1)} collective-permute-done((bf16[512,768]{1,0:T(8,128)(2,1)}, bf16[512,768]{1,0:T(8,128)(2,1)S(1)}, u32[]{:S(2)}, u32[]{:S(2)}) %collective-permute-start.2) | collective-permute-done | bytes 786464 | tf_op jit(solution)/shard_map/ppermute | solution.py:17
  593.1 74.1 %collective-permute-done.3 = bf16[1024,768]{1,0:T(8,128)(2,1)S(1)} collective-permute-done((bf16[1024,768]{1,0:T(8,128)(2,1)}, bf16[1024,768]{1,0:T(8,128)(2,1)S(1)}, u32[]{:S(2)}, u32[]{:S(2)}) %collective-permute-start.3) | collective-permute-done | bytes 1572896 | tf_op jit(solution)/shard_map/ppermute | solution.py:17
  672.9 62.3 %reduce-scatter.20.cloned.1.call-done = bf16[128,768]{1,0:T(8,128)(2,1)} async-done(((bf16[2048,768]{1,0:T(8,128)(2,1)}), bf16[128,768]{1,0:T(8,128)(2,1)}) %reduce-scatter.20.cloned.1.call-update) | async-done | bytes 196624 | tf_op jit(solution)/shard_map/reduce_scatter | solution.py:218
  735.2 69.1 %reduce-scatter.16.cloned.1.call-done = bf16[48,2048]{1,0:T(8,128)(2,1)} async-done(((bf16[768,2048]{1,0:T(8,128)(2,1)}), bf16[48,2048]{1,0:T(8,128)(2,1)}) %reduce-scatter.16.cloned.1.call-update) | async-done | bytes 196624 | tf_op jit(solution)/shard_map/reduce_scatter | solution.py:212
  804.3 69.0 %reduce-scatter.18.cloned.1.call-done = bf16[48,2048]{1,0:T(8,128)(2,1)} async-done(((bf16[768,2048]{1,0:T(8,128)(2,1)}), bf16[48,2048]{1,0:T(8,128)(2,1)}) %reduce-scatter.18.cloned.1.call-update) | async-done | bytes 196624 | tf_op jit(solution)/shard_map/reduce_scatter | solution.py:215
  873.3 8.6 fusion.37
  881.9 29.5 %all-reduce.2 = (bf16[768]{0:T(1024)(128)(2,1)S(1)}, bf16[768]{0:T(1024)(128)(2,1)S(1)}) all-reduce(bf16[768]{0:T(1024)(128)(2,1)S(1)} %get-tuple-element.13, bf16[768]{0:T(1024)(128)(2,1)S(1)} %copy-done.41), channel_id=2, replica_groups=mesh['shard'=16,'replica'=2] {'shard'}, use_global_device_ids=true, to_apply=%region_16.17.clone | all-reduce | flops 1536 | bytes 6144
  921.2 8.6 scatter_custom_fusion
  (216 shorter events, 148.5 us)
Async XLA Ops:
  7.2 59.6 %all-gather.10.cloned.1.call-start = ((), (), s32[]{:S(2)}) async-start(), calls=%async_computation.10 | async-start | bytes 1253376 | tf_op jit(solution)/shard_map/all_gather | solution.py:168
  7.9 95.3 %all-gather.12.cloned.1.call-start = ((), (), s32[]{:S(2)}) async-start(), calls=%async_computation.11 | async-start | bytes 1253376 | tf_op jit(solution)/shard_map/all_gather | solution.py:169
  8.7 143.9 %all-gather.8.cloned.1.call-start = ((), (), s32[]{:S(2)}) async-start(), calls=%async_computation.9 | async-start | bytes 1253376 | tf_op jit(solution)/shard_map/all_gather | solution.py:170
  9.4 172.7 %all-gather.14.cloned.1.call-start = ((), (), s32[]{:S(2)}) async-start(), calls=%async_computation.12 | async-start | bytes 1253376 | tf_op jit(solution)/shard_map/all_gather | solution.py:171
  10.0 218.7 %all-gather.18.cloned.1.call-start = ((), (), s32[]{:S(2)}) async-start(), calls=%async_computation.14 | async-start | bytes 3342336 | tf_op jit(solution)/shard_map/all_gather | solution.py:184
  10.6 264.1 %all-gather.16.cloned.1.call-start = ((), (), s32[]{:S(2)}) async-start(), calls=%async_computation.13 | async-start | bytes 3342336 | tf_op jit(solution)/shard_map/all_gather | solution.py:183
  20.3 44.9 %copy-start.31 = (f32[768]{0:T(1024)S(1)}, f32[768]{0:T(1024)}, u32[]{:S(2)}) copy-start(f32[768]{0:T(1024)} %param.16) | copy-start | bytes 9220
  20.3 44.4 %all-to-all-start = ((bf16[16,64,768]{2,1,0:T(8,128)(2,1)}), bf16[16,64,768]{2,1,0:T(8,128)(2,1)S(1)}, u32[]{:S(2)}, u32[]{:S(2)}) async-start(bf16[16,64,768]{2,1,0:T(8,128)(2,1)} %broadcast_select_fusion), calls=%async_computation | async-start | bytes 3145728 | tf_op jit(solution)/shard_map/all_to_all | solution.py:162
  27.9 292.9 %all-gather.20.cloned.1.call-start = ((), (), s32[]{:S(2)}) async-start(), calls=%async_computation.15 | async-start | bytes 3342336 | tf_op jit(solution)/shard_map/all_gather | solution.py:198
  28.6 644.3 %reduce-scatter.14.cloned.1.call-start = ((), (), s32[]{:S(2)}) async-start(), calls=%async_computation.19 | async-start | bytes 1253376 | tf_op jit(solution)/shard_map/reduce_scatter | solution.py:268
  64.8 120.6 %copy-start.2 = (bf16[16,64,768]{2,1,0:T(8,128)(2,1)}, bf16[16,64,768]{2,1,0:T(8,128)(2,1)S(1)}, u32[]{:S(2)}) copy-start(bf16[16,64,768]{2,1,0:T(8,128)(2,1)S(1)} %all-to-all-done) | copy-start | bytes 4718596
  70.1 36.3 %copy-start.6 = (bf16[512,768]{0,1:T(8,128)(2,1)}, bf16[512,768]{0,1:T(8,128)(2,1)S(1)}, u32[]{:S(2)}) copy-start(bf16[512,768]{0,1:T(8,128)(2,1)S(1)} %get-tuple-element.39) | copy-start | bytes 2359300
  70.1 47.1 %copy-start.14 = (bf16[512,768]{0,1:T(8,128)(2,1)}, bf16[512,768]{0,1:T(8,128)(2,1)S(1)}, u32[]{:S(2)}) copy-start(bf16[512,768]{0,1:T(8,128)(2,1)S(1)} %get-tuple-element.40) | copy-start | bytes 2359300
  187.8 40.9 %copy-start.26 = (bf16[1024,768]{1,0:T(8,128)(2,1)}, bf16[1024,768]{1,0:T(8,128)(2,1)S(1)}, u32[]{:S(2)}) copy-start(bf16[1024,768]{1,0:T(8,128)(2,1)S(1)} %multiply_convert_fusion.5) | copy-start | bytes 4718596
  236.1 84.6 %copy-start.19 = (bf16[1,1,1024,768]{3,2,1,0:T(8,128)(2,1)S(1)}, bf16[1,1,1024,768]{3,2,1,0:T(8,128)(2,1)}, u32[]{:S(2)}) copy-start(bf16[1,1,1024,768]{3,2,1,0:T(8,128)(2,1)} %param.25) | copy-start | bytes 4718596
  320.8 15.1 %copy-start.43 = (bf16[768,2048]{1,0:T(8,128)(2,1)S(1)}, bf16[768,2048]{1,0:T(8,128)(2,1)}, u32[]{:S(2)}) copy-start(bf16[768,2048]{1,0:T(8,128)(2,1)} %all-gather.16.cloned.1.call-done) | copy-start | bytes 9437188
  353.3 319.6 %reduce-scatter.12.cloned.1.call-start = ((), (), s32[]{:S(2)}) async-start(), calls=%async_computation.18 | async-start | bytes 1253376 | tf_op jit(solution)/shard_map/reduce_scatter | solution.py:265
  417.1 13.4 %copy-start.24 = (bf16[16,64,768]{2,1,0:T(8,128)(2,1)S(1)}, bf16[16,64,768]{2,1,0:T(8,128)(2,1)}, u32[]{:S(2)}) copy-start(bf16[16,64,768]{2,1,0:T(8,128)(2,1)} %fusion.31) | copy-start | bytes 4718596
  433.0 239.9 %reduce-scatter.8.cloned.1.call-start = ((), (), s32[]{:S(2)}) async-start(), calls=%async_computation.16 | async-start | bytes 1253376 | tf_op jit(solution)/shard_map/reduce_scatter | solution.py:259
  433.0 42.6 %copy-start.5 = (bf16[1024,768]{0,1:T(8,128)(2,1)S(1)}, bf16[1024,768]{0,1:T(8,128)(2,1)}, u32[]{:S(2)}) copy-start(bf16[1024,768]{0,1:T(8,128)(2,1)} %copy-done.4) | copy-start | bytes 4718596
  496.4 176.5 %reduce-scatter.10.cloned.1.call-start = ((), (), s32[]{:S(2)}) async-start(), calls=%async_computation.17 | async-start | bytes 1253376 | tf_op jit(solution)/shard_map/reduce_scatter | solution.py:262
  514.6 220.6 %reduce-scatter.20.cloned.1.call-start = ((), (), s32[]{:S(2)}) async-start(), calls=%async_computation.22 | async-start | bytes 3342336 | tf_op jit(solution)/shard_map/reduce_scatter | solution.py:218
  522.1 282.2 %reduce-scatter.16.cloned.1.call-start = ((), (), s32[]{:S(2)}) async-start(), calls=%async_computation.20 | async-start | bytes 3342336 | tf_op jit(solution)/shard_map/reduce_scatter | solution.py:212
  530.6 342.7 %reduce-scatter.18.cloned.1.call-start = ((), (), s32[]{:S(2)}) async-start(), calls=%async_computation.21 | async-start | bytes 3342336 | tf_op jit(solution)/shard_map/reduce_scatter | solution.py:215
  531.5 4.9 collective-permute-start
  536.4 12.4 %collective-permute-start.1 = (bf16[256,768]{1,0:T(8,128)(2,1)S(1)}, bf16[256,768]{1,0:T(8,128)(2,1)S(1)}, u32[]{:S(2)}, u32[]{:S(2)}) collective-permute-start(bf16[256,768]{1,0:T(8,128)(2,1)S(1)} %pad_maximum_fusion.8), channel_id=1, source_target_pairs={{0,28},{2,30},{4,0},{6,2},{8,4},{10,6},{12,8},{14,10},{16,12},{18,... | collective-permute-start | bytes 1179656 | tf_op jit(solution)/shard_map/ppermute | solution.py:17
  549.8 20.8 %collective-permute-start.2 = (bf16[512,768]{1,0:T(8,128)(2,1)}, bf16[512,768]{1,0:T(8,128)(2,1)S(1)}, u32[]{:S(2)}, u32[]{:S(2)}) collective-permute-start(bf16[512,768]{1,0:T(8,128)(2,1)} %pad_maximum_fusion.7), channel_id=1, source_target_pairs={{0,24},{2,26},{4,28},{6,30},{8,0},{10,2},{12,4},{14,6},{16,8},{18,... | collective-permute-start | bytes 2359304 | tf_op jit(solution)/shard_map/ppermute | solution.py:17
  571.8 95.4 %collective-permute-start.3 = (bf16[1024,768]{1,0:T(8,128)(2,1)}, bf16[1024,768]{1,0:T(8,128)(2,1)S(1)}, u32[]{:S(2)}, u32[]{:S(2)}) collective-permute-start(bf16[1024,768]{1,0:T(8,128)(2,1)} %pad_maximum_fusion.1), channel_id=1, source_target_pairs={{0,16},{2,18},{4,20},{6,22},{8,24},{10,26},{12,28},{14,30},{16,0},... | collective-permute-start | bytes 4718600 | tf_op jit(solution)/shard_map/ppermute | solution.py:17
  582.8 335.0 %all-to-all-start.1 = ((bf16[16,64,768]{2,1,0:T(8,128)(2,1)}), bf16[16,64,768]{2,1,0:T(8,128)(2,1)}, u32[]{:S(2)}, u32[]{:S(2)}) async-start(bf16[16,64,768]{2,1,0:T(8,128)(2,1)} %bitcast.26), calls=%async_computation.1 | async-start | bytes 3145728 | tf_op jit(solution)/shard_map/all_to_all | solution.py:251
  588.7 342.1 %all-reduce.7.cloned.1.call-start = ((), (), s32[]{:S(2)}) async-start(), calls=%async_computation.23 | async-start | bytes 1769472 | tf_op jit(solution)/shard_map/psum | solution.py:280
  873.3 44.5 %copy-start.38 = (pred[16,64]{1,0:T(8,128)(4,1)S(1)}, pred[16,64]{1,0:T(8,128)(4,1)}, u32[]{:S(2)}) copy-start(pred[16,64]{1,0:T(8,128)(4,1)} %copy-done.37) | copy-start | bytes 3076
  921.2 20.9 %copy-start.1 = (bf16[1,512,768]{2,1,0:T(8,128)(2,1)S(1)}, bf16[1,512,768]{2,1,0:T(8,128)(2,1)}, u32[]{:S(2)}) copy-start(bf16[1,512,768]{2,1,0:T(8,128)(2,1)} %param.13) | copy-start | bytes 2359300
  (38 other events, 153.4 us)
Sparse Core Ops, SparseCore 0:
  10.3 51.5 all-gather.9
  64.1 39.0 all-gather.11
  105.6 37.1 all-gather.7
  144.9 37.1 all-gather.13
  184.2 44.3 all-gather.17
  230.8 43.8 all-gather.15
  276.9 43.8 all-gather.19
  353.4 56.4 reduce-scatter.13
  433.1 56.5 reduce-scatter.11
  496.5 58.0 reduce-scatter.7
  558.2 92.5 reduce-scatter.9
  654.5 80.6 reduce-scatter.19
  739.0 65.2 reduce-scatter.15
  808.0 65.2 reduce-scatter.17
  875.9 35.5 all-reduce.6
